TPU v7x, 256 devices: a whole 4x4x8 slice. The times are simulated.
256 devices in a mesh: wide: 32 (over z, x_lo, core), tm: 8 (over x_hi, y).
Axes of the slice: x: 4 (x_hi: 2, x_lo: 2; x = x_hi * 2 + x_lo), y: 4, z: 8, core: 2. Of those that a mesh axis runs over, the one named last changes fastest.
Arguments:
- clips_in: bfloat16 [32, 32, 14, 14, 256], P('wide', 'tm'), may hold values from -6 to 6
- w_spatial: bfloat16 [3, 3, 256, 256], replicated, may hold values from -0.125 to 0.125
- w_temporal: bfloat16 [3, 256, 256], replicated, may hold values from -0.21875 to 0.21875
- w_proj: bfloat16 [256, 512], replicated, may hold values from -0.375 to 0.375
- prompts: bfloat16 [4096, 512], P('tm'), may hold values from -6 to 6
- positives: int32 [32, 4], P('wide'), may hold values from 0 to 4095
Outputs:
- grad_spatial: float32 [3, 3, 256, 256], replicated
- grad_temporal: float32 [3, 256, 256], replicated
- grad_proj: float32 [256, 512], replicated
- grad_prompts: float32 [4096, 512], P('tm')
Inputs may be any that keep to these rules, and one draw needn't show every extreme that they name: `positives`: 4 positive prompt ids for each clip; a clip may name one id more than once.
All inputs are finite; a program needn't handle non-finite values.
Results may differ from a plain program's by a relative error of at most 0.0037.
Values may be sent and summed in bfloat16 or wider, within the bound.
A program may use at most 64 MiB of HBM per device.

v0:
```python
import jax
import jax.numpy as jnp
from jax import lax
from jax.sharding import PartitionSpec as P

HI = lax.Precision.HIGHEST


def extended(block, sides, width):
    for axis, dim in sides:
        count = lax.axis_size(axis)
        forward = [(i, i + 1) for i in range(count - 1)]
        backward = [(target, source) for source, target in forward]
        low = lax.ppermute(
            lax.slice_in_dim(block, block.shape[dim] - width, None, axis=dim), axis, forward
        )
        high = lax.ppermute(lax.slice_in_dim(block, 0, width, axis=dim), axis, backward)
        block = jnp.concatenate([low, block, high], axis=dim)
    return block


def dsilu(v):
    sig = jax.nn.sigmoid(v)
    return sig * (1.0 + v * (1.0 - sig))


def contract(left, right):
    return lax.dot_general(
        left, right, (((0,), (0,)), ((), ())), preferred_element_type=jnp.float32
    )


def count_hits(pos_ids, ids):
    return jnp.sum((pos_ids[:, :, None] == ids[None, None, :]).astype(jnp.float32), axis=1)


def body(clips_in, w_spatial, w_temporal, w_proj, prompts, positives):
    clips, frames, side, unused, chan = clips_in.shape
    rows = clips * frames * side * side
    padded = jnp.pad(clips_in, ((0, 0), (0, 0), (1, 1), (1, 1), (0, 0)))
    pre_s = jnp.zeros((rows, chan), jnp.float32)
    for a in range(3):
        for b in range(3):
            window = padded[:, :, a : a + side, b : b + side, :].reshape(rows, chan)
            pre_s = pre_s + jnp.dot(window, w_spatial[a, b], preferred_element_type=jnp.float32)
    act = jax.nn.silu(pre_s).astype(jnp.bfloat16).reshape(clips, frames, side, side, chan)
    act_wide = extended(act, (("tm", 1),), 1)
    pre_t = jnp.zeros((rows, chan), jnp.float32)
    for t in range(3):
        pre_t = pre_t + jnp.dot(
            act_wide[:, t : t + frames].reshape(rows, chan),
            w_temporal[t],
            preferred_element_type=jnp.float32,
        )
    out = clips_in.reshape(rows, chan).astype(jnp.float32) + jax.nn.silu(pre_t)
    pooled_loc = jnp.sum(out.reshape(clips, frames * side * side, chan), axis=1)
    pooled = lax.psum(pooled_loc, "tm")
    proj32 = w_proj.astype(jnp.float32)
    z = jnp.dot(pooled, proj32, precision=HI)
    znorm = jnp.sqrt(jnp.sum(z * z, axis=1, keepdims=True) + 1e-06)
    zhat = z / znorm
    p32 = prompts.astype(jnp.float32)
    pnorm = jnp.sqrt(jnp.sum(p32 * p32, axis=1, keepdims=True) + 1e-06)
    phat = p32 / pnorm
    expo = jnp.exp(16.0 * jnp.dot(zhat, phat.T, precision=HI))
    shard = phat.shape[0]
    ids = lax.axis_index("tm") * shard + jnp.arange(shard, dtype=jnp.int32)
    multi = count_hits(positives, ids)
    pos_expo = multi * expo
    total, pos_total = lax.psum(
        (jnp.sum(expo, axis=1, keepdims=True), jnp.sum(pos_expo, axis=1, keepdims=True)), "tm"
    )
    g_s = expo / total - pos_expo / pos_total
    g_zhat = lax.psum(16.0 * jnp.dot(g_s, phat, precision=HI), "tm")
    g_phat = lax.psum(16.0 * jnp.dot(g_s.T, zhat, precision=HI), "wide")
    grad_prompts = (g_phat - phat * jnp.sum(phat * g_phat, axis=1, keepdims=True)) / pnorm
    g_z = (g_zhat - zhat * jnp.sum(zhat * g_zhat, axis=1, keepdims=True)) / znorm
    proj_term = jnp.dot(pooled_loc.T, g_z, precision=HI)
    g_pooled = jnp.dot(g_z, proj32.T, precision=HI)
    g_t = (g_pooled[:, None, :] * dsilu(pre_t).reshape(clips, frames * side * side, chan)).astype(
        jnp.bfloat16
    )
    g_t_flat = g_t.reshape(rows, chan)
    temporal_term = jnp.stack(
        [contract(act_wide[:, t : t + frames].reshape(rows, chan), g_t_flat) for t in range(3)]
    )
    g_wide = extended(g_t.reshape(clips, frames, side, side, chan), (("tm", 1),), 1)
    g_act = jnp.zeros((rows, chan), jnp.float32)
    for t in range(3):
        g_act = g_act + jnp.dot(
            g_wide[:, 2 - t : 2 - t + frames].reshape(rows, chan),
            w_temporal[t].T,
            preferred_element_type=jnp.float32,
        )
    g_sp = (g_act * dsilu(pre_s)).astype(jnp.bfloat16)
    spatial_term = jnp.stack(
        [
            jnp.stack(
                [
                    contract(padded[:, :, a : a + side, b : b + side, :].reshape(rows, chan), g_sp)
                    for b in range(3)
                ]
            )
            for a in range(3)
        ]
    )
    spatial_sum, temporal_sum, proj_sum = lax.psum(
        (spatial_term, temporal_term, proj_term), ("wide", "tm")
    )
    return (spatial_sum, temporal_sum, proj_sum, grad_prompts)


def solution(mesh):
    placed = (P("wide", "tm", None, None, None), P(), P(), P(), P("tm", None), P("wide", None))
    return jax.shard_map(
        body, mesh=mesh, in_specs=placed, out_specs=(P(), P(), P(), P("tm", None)), check_vma=False
    )
```

profile of v0, /device:TPU:8, one launch (start us, length us, event | category | flops | bytes accessed | tf_op | source)
XLA Modules:
  0.0 645.8 jit_solution(18042460652931843559)
XLA Ops:
  7.2 1.1 copy.23
  8.3 3.9 pad_slice_fusion.1
  12.4 1.1 copy.29
  14.2 1.2 copy.27
  15.6 1.2 copy.28
  19.8 1.3 fusion.23
  24.7 1.2 multiply_convert_fusion.1
  26.0 3.5 collective-permute-start
  29.5 2.4 collective-permute-start.1
  32.1 2.1 fusion.11
  34.3 2.1 collective-permute-done.1
  38.3 1.3 fusion.7
  39.6 2.2 add_reduce_fusion
  41.9 20.6 %psum.56 = f32[256]{0:T(256)S(1)} all-reduce(f32[256]{0:T(256)S(1)} %get-tuple-element.29), channel_id=1, replica_groups=mesh['wide'=32,'tm'=8] {'tm'}, use_global_device_ids=true, to_apply=%region_1.2 | all-reduce | flops 256 | bytes 2048 | tf_op jit(solution)/shard_map/psum | solution.py:57
  65.7 22.4 %all-reduce.2 = (f32[]{:T(128)}, f32[]{:T(128)}) all-reduce(f32[]{:T(128)} %get-tuple-element.5, f32[]{:T(128)} %get-tuple-element.4), channel_id=1, replica_groups=mesh['wide'=32,'tm'=8] {'tm'}, use_global_device_ids=true, to_apply=%region_8.9 | all-reduce | flops 2 | bytes 16 | tf_op jit(solution)/shard_map/psum | solution.py:70
  88.1 1.3 divide_subtract_fusion
  90.2 19.0 %psum.59 = f32[1,512]{1,0:T(1,128)S(1)} all-reduce(f32[1,512]{1,0:T(1,128)S(1)} %bitcast.147), channel_id=1, replica_groups=mesh['wide'=32,'tm'=8] {'tm'}, use_global_device_ids=true, to_apply=%region_9.10 | all-reduce | flops 512 | bytes 4096 | tf_op jit(solution)/shard_map/psum | solution.py:74
  110.8 1.4 multiply_convert_fusion
  113.3 1.1 convolution_bitcast_fusion.1
  114.8 2.1 fusion.9
  116.9 1.1 multiply_multiply_fusion
  118.1 7.1 %collective-permute-start.2 = (bf16[1,1,14,14,256]{4,3,2,1,0:T(8,128)(2,1)S(1)}, bf16[1,1,14,14,256]{4,3,2,1,0:T(8,128)(2,1)S(1)}, u32[]{:S(2)}, u32[]{:S(2)}) collective-permute-start(bf16[1,1,14,14,256]{4,3,2,1,0:T(8,128)(2,1)S(1)} %get-tuple-element.13), channel_id=1, source_target_pairs={{1,0},{2,1},{3,2},{4,3},{5,4},{6,5},{7,6},{9,8},{10,9},{11,10},{12... | collective-permute-start | bytes 301064 | tf_op jit(solution)/shard_map/ppermute | solution.py:17
  125.2 1.9 collective-permute-start.3
  129.2 2.6 collective-permute-done.3
  133.0 1.3 fusion.5
  134.5 1.5 fusion.3
  140.6 1.6 pad_maximum_fusion
  142.2 215.7 %all-reduce.6.cloned.1.call-done = f32[512,512]{1,0:T(8,128)} async-done(((f32[512,512]{1,0:T(8,128)}), f32[512,512]{1,0:T(8,128)}) %all-reduce.6.cloned.1.call-update) | async-done | bytes 1048592 | tf_op jit(solution)/shard_map/psum | solution.py:75
  357.9 1.6 multiply_reduce_fusion
  359.5 1.2 subtract_divide_fusion
  360.7 272.8 %all-reduce.8.cloned.1.call-done = (f32[3,3,256,256]{3,2,1,0:T(8,128)}, f32[3,256,256]{2,1,0:T(8,128)}, f32[256,512]{1,0:T(8,128)}) async-done(((f32[3,3,256,256]{3,2,1,0:T(8,128)}, f32[3,256,256]{2,1,0:T(8,128)}, f32[256,512]{1,0:T(8,128)}), (f32[3,3,256,256]{3,2,1,0:T(8,128)}, f32[3,256,256]{2,1,0:T(8,128)}, f32[256,512]{1,0:T(8,128)})) %all-reduce.8.cloned.1.call-update) | async-done | bytes 3670032 | tf_op jit(solution)/shard_map/psum | solution.py:107
  633.5 3.3 copy.37
  (127 shorter events, 26.2 us)
Async XLA Ops:
  7.2 55.3 %copy-start = (bf16[256,512]{1,0:T(8,128)(2,1)S(1)}, bf16[256,512]{1,0:T(8,128)(2,1)}, u32[]{:S(2)}) copy-start(bf16[256,512]{1,0:T(8,128)(2,1)} %param.9) | copy-start | bytes 786436
  7.2 350.7 %all-reduce.6.cloned.1.call-start = ((), (), s32[]{:S(2)}) async-start(), calls=%async_computation | async-start | bytes 2097152 | tf_op jit(solution)/shard_map/psum | solution.py:75
  13.6 10.1 %copy-start.5 = (bf16[784,256]{1,0:T(8,128)(2,1)}, bf16[784,256]{1,0:T(8,128)(2,1)S(1)}, u32[]{:S(2)}) copy-start(bf16[784,256]{1,0:T(8,128)(2,1)S(1)} %reshape.210) | copy-start | bytes 1204228
  14.0 7.6 %copy-start.3 = (bf16[784,256]{1,0:T(8,128)(2,1)}, bf16[784,256]{1,0:T(8,128)(2,1)S(1)}, u32[]{:S(2)}) copy-start(bf16[784,256]{1,0:T(8,128)(2,1)S(1)} %reshape.206) | copy-start | bytes 1204228
  14.2 7.6 %copy-start.7 = (bf16[784,256]{1,0:T(8,128)(2,1)}, bf16[784,256]{1,0:T(8,128)(2,1)S(1)}, u32[]{:S(2)}) copy-start(bf16[784,256]{1,0:T(8,128)(2,1)S(1)} %reshape.207) | copy-start | bytes 1204228
  15.5 6.8 %copy-start.9 = (bf16[784,256]{1,0:T(8,128)(2,1)}, bf16[784,256]{1,0:T(8,128)(2,1)S(1)}, u32[]{:S(2)}) copy-start(bf16[784,256]{1,0:T(8,128)(2,1)S(1)} %reshape.208) | copy-start | bytes 1204228
  19.8 1.8 copy-start.13
  19.8 1.5 copy-start.15
  22.4 1.0 copy-start.11
  23.7 1.0 copy-start.20
  25.9 6.0 copy-start.1
  26.0 8.2 %copy-start.27 = (s32[1,4]{1,0:T(1,128)S(1)}, s32[1,4]{1,0:T(1,128)}, u32[]{:S(2)}) copy-start(s32[1,4]{1,0:T(1,128)} %param.11) | copy-start | bytes 52
  26.0 8.2 %collective-permute-start = (bf16[1,1,14,14,256]{4,3,2,1,0:T(8,128)(2,1)S(1)}, bf16[1,1,14,14,256]{4,3,2,1,0:T(8,128)(2,1)S(1)}, u32[]{:S(2)}, u32[]{:S(2)}) collective-permute-start(bf16[1,1,14,14,256]{4,3,2,1,0:T(8,128)(2,1)S(1)} %get-tuple-element.17), channel_id=1, source_target_pairs={{0,1},{1,2},{2,3},{3,4},{4,5},{5,6},{6,7},{8,9},{9,10},{10,11},{11... | collective-permute-start | bytes 301064 | tf_op jit(solution)/shard_map/ppermute | solution.py:14
  29.5 6.8 %collective-permute-start.1 = (bf16[1,1,14,14,256]{4,3,2,1,0:T(8,128)(2,1)S(1)}, bf16[1,1,14,14,256]{4,3,2,1,0:T(8,128)(2,1)}, u32[]{:S(2)}, u32[]{:S(2)}) collective-permute-start(bf16[1,1,14,14,256]{4,3,2,1,0:T(8,128)(2,1)S(1)} %get-tuple-element.18), channel_id=1, source_target_pairs={{1,0},{2,1},{3,2},{4,3},{5,4},{6,5},{7,6},{9,8},{10,9},{11,10},{12... | collective-permute-start | bytes 301064 | tf_op jit(solution)/shard_map/ppermute | solution.py:17
  38.3 1.3 copy-start.17
  38.3 1.3 copy-start.22
  112.2 2.1 copy-start.23
  118.0 10.3 %copy-start.25 = (f32[1,256,256]{2,1,0:T(8,128)S(1)}, f32[1,256,256]{2,1,0:T(8,128)}, u32[]{:S(2)}) copy-start(f32[1,256,256]{2,1,0:T(8,128)} %convolution_bitcast_fusion) | copy-start | bytes 786436
  118.0 10.3 %copy-start.26 = (f32[1,256,256]{2,1,0:T(8,128)S(1)}, f32[1,256,256]{2,1,0:T(8,128)}, u32[]{:S(2)}) copy-start(f32[1,256,256]{2,1,0:T(8,128)} %convolution_bitcast_fusion.1) | copy-start | bytes 786436
  118.1 11.2 %collective-permute-start.2 = (bf16[1,1,14,14,256]{4,3,2,1,0:T(8,128)(2,1)S(1)}, bf16[1,1,14,14,256]{4,3,2,1,0:T(8,128)(2,1)S(1)}, u32[]{:S(2)}, u32[]{:S(2)}) collective-permute-start(bf16[1,1,14,14,256]{4,3,2,1,0:T(8,128)(2,1)S(1)} %get-tuple-element.13), channel_id=1, source_target_pairs={{1,0},{2,1},{3,2},{4,3},{5,4},{6,5},{7,6},{9,8},{10,9},{11,10},{12... | collective-permute-start | bytes 301064 | tf_op jit(solution)/shard_map/ppermute | solution.py:17
  125.2 6.7 %collective-permute-start.3 = (bf16[1,1,14,14,256]{4,3,2,1,0:T(8,128)(2,1)S(1)}, bf16[1,1,14,14,256]{4,3,2,1,0:T(8,128)(2,1)S(1)}, u32[]{:S(2)}, u32[]{:S(2)}) collective-permute-start(bf16[1,1,14,14,256]{4,3,2,1,0:T(8,128)(2,1)S(1)} %get-tuple-element.14), channel_id=1, source_target_pairs={{0,1},{1,2},{2,3},{3,4},{4,5},{5,6},{6,7},{8,9},{9,10},{10,11},{11... | collective-permute-start | bytes 301064 | tf_op jit(solution)/shard_map/ppermute | solution.py:14
  128.1 505.5 %all-reduce.8.cloned.1.call-start = ((), (), s32[]{:S(2)}) async-start(), calls=%async_computation.1 | async-start | bytes 7340032 | tf_op jit(solution)/shard_map/psum | solution.py:107
  132.9 1.5 copy-start.16
  133.0 1.4 copy-start.24
  133.0 1.5 copy-start.28
  134.5 1.5 copy-start.21
  134.5 1.9 copy-start.6
  136.4 1.0 copy-start.10
  138.1 1.0 copy-start.4
  357.9 1.6 copy-start.2
  633.5 3.3 copy-start.18
  636.8 1.3 copy-start.19
  (3 other events, 3.0 us)
Sparse Core Ops, SparseCore 0:
  128.2 229.6 all-reduce.5
  365.2 268.2 all-reduce.7
where the time goes:
time: 647 us; the launch traced here: 646 us
  waiting for transfers between devices  493 us (76%)
  blocking collectives  62 us (10%)
  local copies, waits for them, and re-layouts  23.1 us (4%)
  matrix products  22.6 us (3%)
  between operations  15.4 us (2%)
  starting transfers between devices  15.2 us (2%)
  other arithmetic  14.3 us (2%)
    psum x1, waiting for transfers between devices, body(): lax.psum((spatial_term, temporal_term, proj_term), ('wide', 'tm'))  273 us
    psum x1, waiting for transfers between devices, body(): g_phat = lax.psum(16.0 * jnp.dot(g_s.T, zhat, precision=HI), 'wide')  216 us
    psum x1, blocking collectives, body(): lax.psum((jnp.sum(expo, axis=1, keepdims=True), jnp.sum(pos_expo, axis=1,...  22.4 us
    psum x1, blocking collectives, body(): pooled = lax.psum(pooled_loc, 'tm')  20.6 us
    psum x1, blocking collectives, body(): g_zhat = lax.psum(16.0 * jnp.dot(g_s, phat, precision=HI), 'tm')  19 us
  transfers between devices with their start and end apart: 6, of which 4 were waited for; matrix products, arithmetic and copies ran while one was open for 2% of the time, Pallas kernels for 0%

commit v1 on v0

--- a/solution.py
+++ b/solution.py
@@ -105,7 +105,7 @@
         ]
     )
     spatial_sum, temporal_sum, proj_sum = lax.psum(
-        (spatial_term, temporal_term, proj_term), ("wide", "tm")
+        lax.psum((spatial_term, temporal_term, proj_term), "wide"), "tm"
     )
     return (spatial_sum, temporal_sum, proj_sum, grad_prompts)
 

time: 647 us -> 514 us (0.79)
  waiting for transfers between devices: 493 us -> 358 us
    psum x2, waiting for transfers between devices: 488 us -> 353 us  [the longest x1 246 us: body(): lax.psum((spatial_term, temporal_term, proj_term), 'wide')]
  transfers between devices with their start and end apart: 6 -> 6, of which waited for: 4 -> 4; matrix products, arithmetic and copies ran while one was open for 2% -> 1% of each run, Pallas kernels for 0% -> 0%
where the time goes in v1:
time: 514 us; the launch traced here: 511 us
  waiting for transfers between devices  358 us (70%)
  blocking collectives  62 us (12%)
  local copies, waits for them, and re-layouts  25 us (5%)
  matrix products  22.7 us (4%)
  between operations  15.3 us (3%)
  starting transfers between devices  15 us (3%)
  other arithmetic  12.9 us (3%)
    psum x1, waiting for transfers between devices, body(): lax.psum((spatial_term, temporal_term, proj_term), 'wide')  246 us
    psum x1, waiting for transfers between devices, body(): lax.psum(lax.psum((spatial_term, temporal_term, proj_term), 'wide'), 'tm')  107 us
    psum x1, blocking collectives, body(): lax.psum((jnp.sum(expo, axis=1, keepdims=True), jnp.sum(pos_expo, axis=1,...  22.4 us
    psum x1, blocking collectives, body(): pooled = lax.psum(pooled_loc, 'tm')  20.6 us
    psum x1, blocking collectives, body(): g_zhat = lax.psum(16.0 * jnp.dot(g_s, phat, precision=HI), 'tm')  19 us
    unnamed x60, local copies, waits for them, and re-layouts  10.3 us
  transfers between devices with their start and end apart: 6, of which 4 were waited for; matrix products, arithmetic and copies ran while one was open for 1% of the time, Pallas kernels for 0%

profile of v1, /device:TPU:8, one launch (start us, length us, event | category | flops | bytes accessed | tf_op | source)
XLA Modules:
  0.0 511.2 jit_solution(11236708159908378469)
XLA Ops:
  7.2 1.1 copy.23
  8.3 4.3 pad_slice_fusion.1
  13.5 1.2 copy.27
  14.9 1.2 copy.28
  17.0 1.1 copy.30
  20.9 1.4 fusion.23
  25.7 1.2 multiply_convert_fusion.1
  27.0 3.5 collective-permute-start
  30.6 2.3 collective-permute-start.1
  33.1 2.1 fusion.11
  35.3 2.1 collective-permute-done.1
  39.4 1.3 fusion.7
  40.7 2.2 add_reduce_fusion
  42.9 20.6 %psum.77 = f32[256]{0:T(256)S(1)} all-reduce(f32[256]{0:T(256)S(1)} %get-tuple-element.33), channel_id=1, replica_groups=mesh['wide'=32,'tm'=8] {'tm'}, use_global_device_ids=true, to_apply=%region_1.2 | all-reduce | flops 256 | bytes 2048 | tf_op jit(solution)/shard_map/psum | solution.py:57
  66.7 22.4 %all-reduce.2 = (f32[]{:T(128)}, f32[]{:T(128)}) all-reduce(f32[]{:T(128)} %get-tuple-element.5, f32[]{:T(128)} %get-tuple-element.4), channel_id=1, replica_groups=mesh['wide'=32,'tm'=8] {'tm'}, use_global_device_ids=true, to_apply=%region_8.9 | all-reduce | flops 2 | bytes 16 | tf_op jit(solution)/shard_map/psum | solution.py:70
  89.1 1.3 divide_subtract_fusion
  91.1 19.0 %psum.80 = f32[1,512]{1,0:T(1,128)S(1)} all-reduce(f32[1,512]{1,0:T(1,128)S(1)} %bitcast.147), channel_id=1, replica_groups=mesh['wide'=32,'tm'=8] {'tm'}, use_global_device_ids=true, to_apply=%region_9.10 | all-reduce | flops 512 | bytes 4096 | tf_op jit(solution)/shard_map/psum | solution.py:74
  111.7 1.4 multiply_convert_fusion
  114.2 1.1 convolution_bitcast_fusion.1
  115.8 2.1 fusion.9
  117.9 1.1 multiply_multiply_fusion
  119.0 7.0 %collective-permute-start.2 = (bf16[1,1,14,14,256]{4,3,2,1,0:T(8,128)(2,1)S(1)}, bf16[1,1,14,14,256]{4,3,2,1,0:T(8,128)(2,1)S(1)}, u32[]{:S(2)}, u32[]{:S(2)}) collective-permute-start(bf16[1,1,14,14,256]{4,3,2,1,0:T(8,128)(2,1)S(1)} %get-tuple-element.17), channel_id=1, source_target_pairs={{1,0},{2,1},{3,2},{4,3},{5,4},{6,5},{7,6},{9,8},{10,9},{11,10},{12... | collective-permute-start | bytes 301064 | tf_op jit(solution)/shard_map/ppermute | solution.py:17
  126.0 2.1 collective-permute-start.3
  129.9 2.7 collective-permute-done.3
  133.8 1.3 fusion.5
  135.3 1.5 fusion.3
  141.1 1.6 pad_maximum_fusion
  142.7 246.1 %all-reduce.7.cloned.1.call-done = (f32[3,3,256,256]{3,2,1,0:T(8,128)}, f32[3,256,256]{2,1,0:T(8,128)}, f32[256,512]{1,0:T(8,128)}, f32[512,512]{1,0:T(8,128)}) async-done(((f32[3,3,256,256]{3,2,1,0:T(8,128)}, f32[3,256,256]{2,1,0:T(8,128)}, f32[256,512]{1,0:T(8,128)}, f32[512,512]{1,0:T(8,128)}), (f32[3,3,256,256]{3,2,1,0:T(8,128)}, f32[3,256,256]{2,1,0:T(8,128)}, f32[256,512]{1,0:T(8,128)}, ...) | async-done | bytes 4718608 | tf_op jit(solution)/shard_map/psum | solution.py:108
  388.9 1.2 copy-done.2
  390.4 1.2 subtract_divide_fusion
  391.6 107.3 %all-reduce.9.cloned.1.call-done = (f32[3,3,256,256]{3,2,1,0:T(8,128)}, f32[3,256,256]{2,1,0:T(8,128)}, f32[256,512]{1,0:T(8,128)}) async-done(((f32[3,3,256,256]{3,2,1,0:T(8,128)}, f32[3,256,256]{2,1,0:T(8,128)}, f32[256,512]{1,0:T(8,128)}), (f32[3,3,256,256]{3,2,1,0:T(8,128)}, f32[3,256,256]{2,1,0:T(8,128)}, f32[256,512]{1,0:T(8,128)})) %all-reduce.9.cloned.1.call-update) | async-done | bytes 3670032 | tf_op jit(solution)/shard_map/psum | solution.py:107
  498.9 3.3 copy.40
  (125 shorter events, 26.6 us)
Async XLA Ops:
  7.2 56.4 %copy-start = (bf16[256,512]{1,0:T(8,128)(2,1)S(1)}, bf16[256,512]{1,0:T(8,128)(2,1)}, u32[]{:S(2)}) copy-start(bf16[256,512]{1,0:T(8,128)(2,1)} %param.9) | copy-start | bytes 786436
  7.2 381.7 %all-reduce.7.cloned.1.call-start = ((), (), s32[]{:S(2)}) async-start(), calls=%async_computation | async-start | bytes 9437184 | tf_op jit(solution)/shard_map/psum | solution.py:108
  12.9 11.8 %copy-start.5 = (bf16[784,256]{1,0:T(8,128)(2,1)}, bf16[784,256]{1,0:T(8,128)(2,1)S(1)}, u32[]{:S(2)}) copy-start(bf16[784,256]{1,0:T(8,128)(2,1)S(1)} %reshape.210) | copy-start | bytes 1204228
  13.3 9.3 %copy-start.3 = (bf16[784,256]{1,0:T(8,128)(2,1)}, bf16[784,256]{1,0:T(8,128)(2,1)S(1)}, u32[]{:S(2)}) copy-start(bf16[784,256]{1,0:T(8,128)(2,1)S(1)} %reshape.206) | copy-start | bytes 1204228
  13.5 9.3 %copy-start.7 = (bf16[784,256]{1,0:T(8,128)(2,1)}, bf16[784,256]{1,0:T(8,128)(2,1)S(1)}, u32[]{:S(2)}) copy-start(bf16[784,256]{1,0:T(8,128)(2,1)S(1)} %reshape.207) | copy-start | bytes 1204228
  14.9 8.5 %copy-start.9 = (bf16[784,256]{1,0:T(8,128)(2,1)}, bf16[784,256]{1,0:T(8,128)(2,1)S(1)}, u32[]{:S(2)}) copy-start(bf16[784,256]{1,0:T(8,128)(2,1)S(1)} %reshape.208) | copy-start | bytes 1204228
  20.8 1.5 copy-start.14
  23.4 1.0 copy-start.11
  24.7 1.0 copy-start.19
  26.9 6.0 %copy-start.1 = (bf16[512,512]{1,0:T(8,128)(2,1)S(1)}, bf16[512,512]{1,0:T(8,128)(2,1)}, u32[]{:S(2)}) copy-start(bf16[512,512]{1,0:T(8,128)(2,1)} %param.10) | copy-start | bytes 1572868
  27.0 8.2 %copy-start.26 = (s32[1,4]{1,0:T(1,128)S(1)}, s32[1,4]{1,0:T(1,128)}, u32[]{:S(2)}) copy-start(s32[1,4]{1,0:T(1,128)} %param.11) | copy-start | bytes 52
  27.0 8.2 %collective-permute-start = (bf16[1,1,14,14,256]{4,3,2,1,0:T(8,128)(2,1)S(1)}, bf16[1,1,14,14,256]{4,3,2,1,0:T(8,128)(2,1)S(1)}, u32[]{:S(2)}, u32[]{:S(2)}) collective-permute-start(bf16[1,1,14,14,256]{4,3,2,1,0:T(8,128)(2,1)S(1)} %get-tuple-element.21), channel_id=1, source_target_pairs={{0,1},{1,2},{2,3},{3,4},{4,5},{5,6},{6,7},{8,9},{9,10},{10,11},{11... | collective-permute-start | bytes 301064 | tf_op jit(solution)/shard_map/ppermute | solution.py:14
  30.6 6.8 %collective-permute-start.1 = (bf16[1,1,14,14,256]{4,3,2,1,0:T(8,128)(2,1)S(1)}, bf16[1,1,14,14,256]{4,3,2,1,0:T(8,128)(2,1)}, u32[]{:S(2)}, u32[]{:S(2)}) collective-permute-start(bf16[1,1,14,14,256]{4,3,2,1,0:T(8,128)(2,1)S(1)} %get-tuple-element.22), channel_id=1, source_target_pairs={{1,0},{2,1},{3,2},{4,3},{5,4},{6,5},{7,6},{9,8},{10,9},{11,10},{12... | collective-permute-start | bytes 301064 | tf_op jit(solution)/shard_map/ppermute | solution.py:17
  39.4 1.3 copy-start.16
  39.4 1.3 copy-start.21
  113.1 2.1 copy-start.22
  117.9 11.1 %copy-start.24 = (f32[1,256,256]{2,1,0:T(8,128)S(1)}, f32[1,256,256]{2,1,0:T(8,128)}, u32[]{:S(2)}) copy-start(f32[1,256,256]{2,1,0:T(8,128)} %convolution_bitcast_fusion) | copy-start | bytes 786436
  117.9 11.1 %copy-start.25 = (f32[1,256,256]{2,1,0:T(8,128)S(1)}, f32[1,256,256]{2,1,0:T(8,128)}, u32[]{:S(2)}) copy-start(f32[1,256,256]{2,1,0:T(8,128)} %convolution_bitcast_fusion.1) | copy-start | bytes 786436
  119.0 10.9 %collective-permute-start.2 = (bf16[1,1,14,14,256]{4,3,2,1,0:T(8,128)(2,1)S(1)}, bf16[1,1,14,14,256]{4,3,2,1,0:T(8,128)(2,1)S(1)}, u32[]{:S(2)}, u32[]{:S(2)}) collective-permute-start(bf16[1,1,14,14,256]{4,3,2,1,0:T(8,128)(2,1)S(1)} %get-tuple-element.17), channel_id=1, source_target_pairs={{1,0},{2,1},{3,2},{4,3},{5,4},{6,5},{7,6},{9,8},{10,9},{11,10},{12... | collective-permute-start | bytes 301064 | tf_op jit(solution)/shard_map/ppermute | solution.py:17
  126.0 6.7 %collective-permute-start.3 = (bf16[1,1,14,14,256]{4,3,2,1,0:T(8,128)(2,1)S(1)}, bf16[1,1,14,14,256]{4,3,2,1,0:T(8,128)(2,1)S(1)}, u32[]{:S(2)}, u32[]{:S(2)}) collective-permute-start(bf16[1,1,14,14,256]{4,3,2,1,0:T(8,128)(2,1)S(1)} %get-tuple-element.18), channel_id=1, source_target_pairs={{0,1},{1,2},{2,3},{3,4},{4,5},{5,6},{6,7},{8,9},{9,10},{10,11},{11... | collective-permute-start | bytes 301064 | tf_op jit(solution)/shard_map/ppermute | solution.py:14
  133.7 1.5 copy-start.15
  133.8 1.4 copy-start.23
  133.8 1.5 copy-start.27
  135.3 1.5 copy-start.20
  135.3 1.9 copy-start.6
  136.8 1.0 copy-start.12
  137.1 1.0 copy-start.10
  138.5 1.0 copy-start.4
  142.7 356.2 %all-reduce.9.cloned.1.call-start = ((), (), s32[]{:S(2)}) async-start(), calls=%async_computation.1 | async-start | bytes 7340032 | tf_op jit(solution)/shard_map/psum | solution.py:107
  388.9 1.2 copy-start.2
  498.9 3.3 copy-start.17
  502.2 1.3 copy-start.18
  (2 other events, 2.0 us)
Sparse Core Ops, SparseCore 0:
  142.8 246.0 all-reduce.6
  391.7 107.1 all-reduce.8
